TPU v7x, 512 devices: a whole 4x4x16 slice. The times are simulated.
512 devices in a mesh: tiles: 128 (over z, y, core), rep: 4 (over x).
Axes of the slice: x: 4, y: 4, z: 16, core: 2. Of those that a mesh axis runs over, the one named last changes fastest.
Arguments:
- tiles: bfloat16 [1024, 64, 4096], P(('tiles', 'rep')), may hold values from -6 to 6
- block_one: int32 [1024], P(('tiles', 'rep')), may hold values from 0 to 127
- block_two: int32 [1024], P(('tiles', 'rep')), may hold values from 0 to 255
- block_three: int32 [1024], P(('tiles', 'rep')), may hold values from 0 to 15
- owner_map: int32 [128], replicated, may hold values from 0 to 127, each once
- u_one: float32 [32, 8192], P(None, 'tiles'), may hold values from -6 to 6
- u_two: bfloat16 [32, 16384], P(None, 'tiles'), may hold values from -6 to 6
- u_three: bfloat16 [32, 1024], replicated, may hold values from -6 to 6
Outputs:
- factor: float32 [32, 8192], P(None, 'tiles')
- tile_factor: bfloat16 [1024, 2048], P(('tiles', 'rep'))
All inputs are finite; a program needn't handle non-finite values.
Results may differ from a plain program's by a relative error of at most 0.0081.
Values may be sent and summed in bfloat16 or wider, within the bound.
A program may use at most 64 MiB of HBM per device.

v0:
```python
import jax
import jax.numpy as jnp
from jax import lax
from jax.sharding import PartitionSpec as P

NS_STEPS = 2


def pick(table, index, width):
    grid = table.reshape(table.shape[0], -1, width)
    return jnp.transpose(jnp.take(grid, index, axis=1), (1, 0, 2))


def gram_total(local):
    return lax.psum(local, "tiles")


def orthonormal(rows, rows_total):
    hi = lax.Precision.HIGHEST
    rank = rows.shape[0]
    g0 = gram_total(jnp.dot(rows, rows.T, precision=hi, preferred_element_type=jnp.float32))
    msq = jnp.trace(g0) / rows_total
    inv = 1.0 / jnp.sqrt(msq + 1e-06)
    x = rows * inv
    g = g0 * (inv * inv) / rows_total
    eye = jnp.eye(rank, dtype=jnp.float32)
    for step in range(NS_STEPS):
        if step > 0:
            g = (
                gram_total(jnp.dot(x, x.T, precision=hi, preferred_element_type=jnp.float32))
                / rows_total
            )
        x = jnp.dot(1.5 * eye - 0.5 * g, x, precision=hi, preferred_element_type=jnp.float32)
    return x


def spread(current):
    cast = current.astype(jnp.bfloat16)
    return lax.all_gather(cast, "tiles", axis=1, tiled=True)


def per_device(tiles, block_one, block_two, block_three, owner_map, u_one, u_two, u_three):
    hi = lax.Precision.HIGHEST
    count = tiles.shape[0]
    width = tiles.shape[1]
    rank = u_three.shape[0]
    blocks_total = owner_map.shape[0]
    rows_total = blocks_total * width
    two_full = lax.all_gather(u_two, "tiles", axis=1, tiled=True)
    two_pick = pick(two_full, block_two, width)
    three_pick = pick(u_three, block_three, width)
    cube = tiles.reshape(count, width, width, width)
    first = jnp.einsum(
        "tijk,tsk->tijs", cube, three_pick, preferred_element_type=jnp.float32
    ).astype(jnp.bfloat16)
    second = jnp.einsum("tijs,trj->tirs", first, two_pick, preferred_element_type=jnp.float32)
    products = second.reshape(count, width, rank * rank).astype(jnp.bfloat16)
    positions = jnp.take(owner_map, block_one)
    onehot = (positions[:, None] == jnp.arange(blocks_total, dtype=jnp.int32)[None, :]).astype(
        jnp.float32
    )
    current = u_one
    readers = pick(spread(current), positions, width)
    partial_value = jnp.einsum("tic,tri->rc", products, readers, preferred_element_type=jnp.float32)
    project = lax.psum(partial_value, ("tiles", "rep")).astype(jnp.bfloat16)
    z_tile = jnp.einsum("rc,tic->tri", project, products, preferred_element_type=jnp.float32)
    term = jnp.einsum("tri,tn->rni", z_tile, onehot, precision=hi).reshape(rank, rows_total)
    rows = lax.psum_scatter(term, "tiles", scatter_dimension=1, tiled=True)
    rows = lax.psum(rows, "rep")
    current = orthonormal(rows, rows_total)
    tile_factor = pick(spread(current), positions, width).reshape(count, rank * width)
    return (current, tile_factor)


def solution(mesh):
    in_specs = (
        P(("tiles", "rep"), None, None),
        P(("tiles", "rep")),
        P(("tiles", "rep")),
        P(("tiles", "rep")),
        P(),
        P(None, "tiles"),
        P(None, "tiles"),
        P(),
    )
    out_specs = (P(None, "tiles"), P(("tiles", "rep"), None))
    return jax.shard_map(
        per_device, mesh=mesh, in_specs=in_specs, out_specs=out_specs, check_vma=False
    )
```

profile of v0, /device:TPU:1, one launch (start us, length us, event | category | flops | bytes accessed | tf_op | source)
XLA Modules:
  0.0 1633.5 jit_solution(5011610970250502089)
XLA Ops:
  8.6 0.7 convert_bitcast_fusion.1
  9.3 1.0 reshape.51
  10.4 109.1 %all-gather = bf16[128,64,32]{1,2,0:T(8,128)(2,1)S(1)} all-gather(bf16[1,64,32]{1,2,0:T(8,128)(2,1)S(1)} %convert_bitcast_fusion.1), channel_id=1, replica_groups=mesh['tiles'=128,'rep'=4] {'tiles'}, dimensions={0}, use_global_device_ids=true | all-gather | bytes 528384 | tf_op jit(solution)/shard_map/all_gather | solution.py:39
  119.9 0.8 reshape.103
  120.7 1.1 reshape.53
  122.6 3.4 reshape.52
  128.0 2.0 fusion
  130.0 17.5 %all-gather.4.cloned.1.call-done = bf16[32,16384]{1,0:T(8,128)(2,1)} async-done(((bf16[32,128]{1,0:T(8,128)(2,1)}), bf16[32,16384]{1,0:T(8,128)(2,1)}) %all-gather.4.cloned.1.call-update) | async-done | bytes 1048592 | tf_op jit(solution)/shard_map/all_gather | solution.py:49
  147.5 3.0 reshape.50
  150.6 2.7 copy.27
  153.3 2.1 gather_fusion.1
  155.4 1.1 fusion.1
  157.0 102.8 %all-reduce.1 = bf16[32,1024]{1,0:T(8,128)(2,1)S(1)} all-reduce(f32[32,1024]{1,0:T(8,128)S(1)} %convolution_bitcast_fusion.1), channel_id=1, replica_groups=mesh['tiles'=128,'rep'=4] {'tiles','rep'}, use_global_device_ids=true, to_apply=%region_0.0 | all-reduce | flops 32768 | bytes 196608 | tf_op jit(solution)/shard_map/psum | solution.py:65
  259.9 1.0 convolution_bitcast_fusion
  261.0 4.4 copy.45
  265.5 245.9 %reduce-scatter.4.cloned.1.call-done = f32[64,32]{1,0:T(8,128)} async-done(((f32[8192,32]{1,0:T(8,128)}), f32[64,32]{1,0:T(8,128)}) %reduce-scatter.4.cloned.1.call-update) | async-done | bytes 8208
  511.3 0.8 copy.44
  512.2 13.3 psum.29
  525.6 500.6 %psum.30 = f32[32,32]{1,0:T(8,128)S(1)} all-reduce(f32[32,32]{1,0:T(8,128)S(1)} %fusion.44), channel_id=1, replica_groups=mesh['tiles'=128,'rep'=4] {'tiles'}, use_global_device_ids=true, to_apply=%region_3.5 | all-reduce | flops 1024 | bytes 8192 | tf_op jit(solution)/shard_map/psum | solution.py:15
  1027.9 490.9 %psum.31 = f32[32,32]{1,0:T(8,128)S(1)} all-reduce(f32[32,32]{1,0:T(8,128)S(1)} %fusion.45), channel_id=1, replica_groups=mesh['tiles'=128,'rep'=4] {'tiles'}, use_global_device_ids=true, to_apply=%region_5.7 | all-reduce | flops 1024 | bytes 8192 | tf_op jit(solution)/shard_map/psum | solution.py:15
  1518.9 103.3 %all-gather.1 = bf16[128,64,32]{1,2,0:T(8,128)(2,1)S(1)} all-gather(bf16[1,64,32]{1,2,0:T(8,128)(2,1)S(1)} %convert_bitcast_fusion), channel_id=1, replica_groups=mesh['tiles'=128,'rep'=4] {'tiles'}, dimensions={0}, use_global_device_ids=true | all-gather | bytes 528384 | tf_op jit(solution)/shard_map/all_gather | solution.py:39
  1622.6 0.8 reshape.105
  1623.5 1.1 reshape.55
  1625.9 0.7 reshape.56
  (44 shorter events, 8.0 us)
Async XLA Ops:
  7.2 118.9 %copy-start = (s32[128]{0:T(128)S(1)}, s32[128]{0:T(128)}, u32[]{:S(2)}) copy-start(s32[128]{0:T(128)} %param.14) | copy-start | bytes 1540
  7.2 140.3 %all-gather.4.cloned.1.call-start = ((), (), s32[]{:S(2)}) async-start(), calls=%async_computation.1 | async-start | bytes 1056768 | tf_op jit(solution)/shard_map/all_gather | solution.py:49
  7.9 503.4 %reduce-scatter.4.cloned.1.call-start = ((), (), s32[]{:S(2)}) async-start(), calls=%async_computation.2 | async-start | bytes 4227072
  122.6 4.2 copy-start.4
  122.6 4.7 copy-start.2
  122.6 5.3 copy-start.3
  1518.9 104.6 %copy-start.1 = (f32[32,64]{1,0:T(8,128)}, f32[32,64]{1,0:T(8,128)S(1)}, u32[]{:S(2)}) copy-start(f32[32,64]{1,0:T(8,128)S(1)} %fusion.7) | copy-start | bytes 24580
Sparse Core Ops, SparseCore 0:
  11.0 136.4 all-gather.3
  265.6 245.7 reduce-scatter.3
where the time goes:
time: 1630 us
  blocking collectives  1320 us (81%)
  waiting for transfers between devices  264 us (16%)
  local copies, waits for them, and re-layouts  27 us (2%)
    psum x2, blocking collectives, gram_total(): return lax.psum(local, 'tiles')  992 us
    unnamed x3, waiting for transfers between devices  247 us
    all_gather x2, blocking collectives, spread(): return lax.all_gather(cast, 'tiles', axis=1, tiled=True)  212 us
    psum x1, blocking collectives, per_device(): project = lax.psum(partial_value, ('tiles', 'rep')).astype(jnp.bfloat16)  103 us
  transfers between devices with their start and end apart: 2, of which 2 were waited for; matrix products, arithmetic and copies ran while one was open for 1% of the time, Pallas kernels for 0%

commit v1 on v0

--- a/solution.py
+++ b/solution.py
@@ -62,7 +62,7 @@
     current = u_one
     readers = pick(spread(current), positions, width)
     partial_value = jnp.einsum("tic,tri->rc", products, readers, preferred_element_type=jnp.float32)
-    project = lax.psum(partial_value, ("tiles", "rep")).astype(jnp.bfloat16)
+    project = lax.psum(lax.psum(partial_value, "tiles"), "rep").astype(jnp.bfloat16)
     z_tile = jnp.einsum("rc,tic->tri", project, products, preferred_element_type=jnp.float32)
     term = jnp.einsum("tri,tn->rni", z_tile, onehot, precision=hi).reshape(rank, rows_total)
     rows = lax.psum_scatter(term, "tiles", scatter_dimension=1, tiled=True)

time: 1630 us -> 1860 us (1.14)
  waiting for transfers between devices: 264 us -> 581 us
  blocking collectives: 1320 us -> 1230 us
    psum x0 -> x1, waiting for transfers between devices: none -> 313 us  [per_device(): lax.psum(partial_value, 'tiles')]
    psum x1, blocking collectives: 103 us -> 15 us  [per_device(): lax.psum(lax.psum(partial_value, 'tiles'), 'rep').astype(jnp.bfloat16)]
    unnamed x3 -> x4, waiting for transfers between devices: 247 us -> 250 us
  transfers between devices with their start and end apart: 2 -> 3, of which waited for: 2 -> 3; matrix products, arithmetic and copies ran while one was open for 1% -> 1% of each run, Pallas kernels for 0% -> 0%
where the time goes in v1:
time: 1860 us
  blocking collectives  1230 us (66%)
  waiting for transfers between devices  581 us (31%)
  local copies, waits for them, and re-layouts  27 us (1%)
    psum x2, blocking collectives, gram_total(): return lax.psum(local, 'tiles')  992 us
    psum x1, waiting for transfers between devices, per_device(): lax.psum(partial_value, 'tiles')  313 us
    unnamed x4, waiting for transfers between devices  250 us
    all_gather x2, blocking collectives, spread(): return lax.all_gather(cast, 'tiles', axis=1, tiled=True)  212 us
  transfers between devices with their start and end apart: 3, of which 3 were waited for; matrix products, arithmetic and copies ran while one was open for 1% of the time, Pallas kernels for 0%

profile of v1, /device:TPU:1, one launch (start us, length us, event | category | flops | bytes accessed | tf_op | source)
XLA Modules:
  0.0 1862.7 jit_solution(9982444385891303892)
XLA Ops:
  9.3 1.0 reshape.51
  10.4 109.1 %all-gather = bf16[128,64,32]{1,2,0:T(8,128)(2,1)S(1)} all-gather(bf16[1,64,32]{1,2,0:T(8,128)(2,1)S(1)} %convert_bitcast_fusion.1), channel_id=1, replica_groups=mesh['tiles'=128,'rep'=4] {'tiles'}, dimensions={0}, use_global_device_ids=true | all-gather | bytes 528384 | tf_op jit(solution)/shard_map/all_gather | solution.py:39
  119.9 0.8 reshape.103
  120.7 1.1 reshape.53
  122.6 3.4 reshape.52
  128.0 2.0 fusion
  130.0 17.5 all-gather.4.cloned.1.call-done
  147.5 3.0 reshape.50
  150.6 2.7 copy.27
  153.3 2.1 gather_fusion.1
  155.4 1.1 fusion.1
  156.7 0.9 convolution_bitcast_fusion.1
  157.7 313.3 %all-reduce.3.cloned.1.call-done = f32[32,1024]{1,0:T(8,128)} async-done(((f32[32,1024]{1,0:T(8,128)}), f32[32,1024]{1,0:T(8,128)}) %all-reduce.3.cloned.1.call-update) | async-done | bytes 131088 | tf_op jit(solution)/shard_map/psum | solution.py:65
  471.0 15.0 all-reduce.4
  486.2 1.0 convolution_bitcast_fusion
  487.3 4.4 copy.45
  491.8 249.0 %reduce-scatter.4.cloned.1.call-done = f32[64,32]{1,0:T(8,128)} async-done(((f32[8192,32]{1,0:T(8,128)}), f32[64,32]{1,0:T(8,128)}) %reduce-scatter.4.cloned.1.call-update) | async-done | bytes 8208
  740.8 0.8 copy.44
  741.6 13.4 psum.37
  755.2 500.6 %psum.38 = f32[32,32]{1,0:T(8,128)S(1)} all-reduce(f32[32,32]{1,0:T(8,128)S(1)} %fusion.44), channel_id=1, replica_groups=mesh['tiles'=128,'rep'=4] {'tiles'}, use_global_device_ids=true, to_apply=%region_4.6 | all-reduce | flops 1024 | bytes 8192 | tf_op jit(solution)/shard_map/psum | solution.py:15
  1257.4 490.9 %psum.39 = f32[32,32]{1,0:T(8,128)S(1)} all-reduce(f32[32,32]{1,0:T(8,128)S(1)} %fusion.45), channel_id=1, replica_groups=mesh['tiles'=128,'rep'=4] {'tiles'}, use_global_device_ids=true, to_apply=%region_6.8 | all-reduce | flops 1024 | bytes 8192 | tf_op jit(solution)/shard_map/psum | solution.py:15
  1748.4 103.3 %all-gather.1 = bf16[128,64,32]{1,2,0:T(8,128)(2,1)S(1)} all-gather(bf16[1,64,32]{1,2,0:T(8,128)(2,1)S(1)} %convert_bitcast_fusion), channel_id=1, replica_groups=mesh['tiles'=128,'rep'=4] {'tiles'}, dimensions={0}, use_global_device_ids=true | all-gather | bytes 528384 | tf_op jit(solution)/shard_map/all_gather | solution.py:39
  1852.1 0.8 reshape.105
  1853.0 1.1 reshape.55
  (47 shorter events, 9.2 us)
Async XLA Ops:
  7.2 118.9 %copy-start = (s32[128]{0:T(128)S(1)}, s32[128]{0:T(128)}, u32[]{:S(2)}) copy-start(s32[128]{0:T(128)} %param.14) | copy-start | bytes 1540
  7.2 140.3 %all-gather.4.cloned.1.call-start = ((), (), s32[]{:S(2)}) async-start(), calls=%async_computation.1 | async-start | bytes 1056768 | tf_op jit(solution)/shard_map/all_gather | solution.py:49
  7.9 463.1 %all-reduce.3.cloned.1.call-start = ((), (), s32[]{:S(2)}) async-start(), calls=%async_computation.2 | async-start | bytes 262144 | tf_op jit(solution)/shard_map/psum | solution.py:65
  122.6 4.2 copy-start.4
  122.6 4.7 copy-start.2
  122.6 5.3 copy-start.3
  157.7 583.1 %reduce-scatter.4.cloned.1.call-start = ((), (), s32[]{:S(2)}) async-start(), calls=%async_computation.3 | async-start | bytes 4227072
  1748.4 104.6 %copy-start.1 = (f32[32,64]{1,0:T(8,128)}, f32[32,64]{1,0:T(8,128)S(1)}, u32[]{:S(2)}) copy-start(f32[32,64]{1,0:T(8,128)S(1)} %fusion.7) | copy-start | bytes 24580
Sparse Core Ops, SparseCore 0:
  11.0 136.4 all-gather.3
  157.8 313.1 all-reduce.2
  491.9 248.8 reduce-scatter.3
